TPU v7x, 512 devices: a whole 4x4x16 slice. The times are simulated.
512 devices in a mesh: op: 4 (over y_lo, core), cell: 128 (over x, y_hi, z).
Axes of the slice: x: 4, y: 4 (y_hi: 2, y_lo: 2; y = y_hi * 2 + y_lo), z: 16, core: 2. Of those that a mesh axis runs over, the one named last changes fastest.
Arguments:
- flow_state: float32 [8, 5, 5, 65536], P('op', None, None, 'cell'), may hold values from -6 to 6
- adjoint_start: float32 [8, 5, 5, 65536], P('op', None, None, 'cell'), may hold values from -6 to 6
- objective_grad: float32 [8, 5, 5, 65536], P('op', None, None, 'cell'), may hold values from -6 to 6
- adjacency: int32 [6, 65536], P(None, 'cell'), may hold values from -1 to 767, as said below
- send_list: int32 [32768], P('cell'), may hold values from 0 to 511, as said below
- cell_nodes: int32 [8, 65536], P(None, 'cell'), may hold values from 0 to 1023, as said below
- coords: float32 [3, 131072], P(None, ('op', 'cell')), may hold values from -0.2 to 32.2, as said below
- jacobians: float32 [8, 3, 5, 5], P('op'), may hold values from -1.5 to 1.5
- dissipation: float32 [8], P('op'), may hold values from 0.3 to 3
- frequency: float32 [8], P('op'), may hold values from 0.5 to 4
Outputs:
- adjoint_out: float32 [8, 5, 5, 65536], P('op', None, None, 'cell')
- node_sens: float32 [3, 131072], P(None, ('op', 'cell'))
Inputs may be any that keep to these rules, and one draw needn't show every extreme that they name: `adjacency`: each block's cells are a lattice of 4 x 32 x 4 cells in some order; slots 0 and 1 face the previous and next circumferential layer, 2 and 3 along the span, 4 and 5 along the axis. An entry under 512 is a cell of the same block; 512 + p with p < 128 is position 128 + p of the previous block's send list, 640 + p is position p of the next block's, the blocks closing into a cycle; -1 is a wall. Only slots 0 and 1 name such entries. Every face is listed by both of its cells: when slot k of cell i names cell j, slot k xor 1 of j names i. `send_list`: each block's 128 first entries are distinct local cells whose slot 0 leaves the block, its 128 last entries those whose slot 1 does. `cell_nodes`: corner c = 4 e1 + 2 e2 + e3 of a cell lies on its side of slot 1 if e1 = 1, else of slot 0, likewise e2 for slots 2 and 3 and e3 for slots 4 and 5. Cells of one block that share a face share its four node slots. `coords`: each node slot that a cell names holds a point within 0.2 in each coordinate of its lattice point, cells being unit cubes of the lattice; other slots hold arbitrary values.
All inputs are finite; a program needn't handle non-finite values.
Results may differ from a plain program's by a relative error of at most 0.00026.
Values sent between devices are 32-bit elements; how exact they have to be, the bound alone decides.
A program may use at most 64 MiB of HBM per device.

v0:
```python
import functools
import math

import jax
import jax.numpy as jnp
import numpy as np
from jax import lax
from jax.experimental import pallas as pl
from jax.experimental.pallas import tpu as pltpu
from jax.sharding import PartitionSpec as P

ITERS = 4
INST = 5
VARS = 5
OPS_HERE = 2
N_OP = 4
LANES = 128
CELLS_HERE = 512
FACE_CORNERS = ((0, 1, 3, 2), (4, 6, 7, 5), (0, 4, 5, 1), (2, 3, 7, 6), (0, 2, 6, 4), (1, 5, 7, 3))
COURANT = 1.2
WEIGHT = 1.0 / 8
STATE = INST * VARS
GROUPS = (STATE + 3) // 4
MESH = pl.DeviceIdType.MESH


def spectral_values():
    values = np.zeros((INST, INST))
    for t in range(INST):
        for s in range(INST):
            if t != s:
                values[t, s] = 0.5 * (-1.0) ** (t - s) / math.sin(math.pi * (t - s) / INST)
    return values


def lanes_at(table, index):
    return jnp.take_along_axis(table, index, axis=1, mode="promise_in_bounds")


def split3(x):
    hi = x.astype(jnp.bfloat16)
    rest = x - hi.astype(jnp.float32)
    mid = rest.astype(jnp.bfloat16)
    low = (rest - mid.astype(jnp.float32)).astype(jnp.bfloat16)
    return jnp.concatenate([hi, mid, low], axis=0)


def move_cells(x, onehot, contract):
    rows = x.shape[0]
    y = lax.dot_general(
        split3(x), onehot, (((1,), (contract,)), ((), ())), preferred_element_type=jnp.float32
    )
    return y[:rows] + y[rows : 2 * rows] + y[2 * rows :]


def spread(row):
    return jnp.broadcast_to(row, (8, LANES))


def cross(a, b):
    return [a[1] * b[2] - a[2] * b[1], a[2] * b[0] - a[0] * b[2], a[0] * b[1] - a[1] * b[0]]


def kernel(
    state_ref,
    start_ref,
    objective_ref,
    adjacency_ref,
    send_ref,
    nodes_ref,
    coords_ref,
    jac_ref,
    damp_ref,
    freq_ref,
    out_ref,
    sens_ref,
    cbuf,
    nodebuf,
    cornerbuf,
    stack,
    lattice,
    corner_lat,
    slot_lat,
    up_send,
    down_send,
    low_recv,
    high_recv,
    rs_send,
    rs_recv,
    outbuf,
    c_send_sem,
    c_recv_sem,
    r_send_sem,
    r_recv_sem,
    up_send_sem,
    up_recv_sem,
    down_send_sem,
    down_recv_sem,
):
    op = lax.axis_index("op")
    cell = lax.axis_index("cell")
    n_cell = 128
    nxt = lax.rem(cell + 1, n_cell)
    prv = lax.rem(cell + n_cell - 1, n_cell)
    peers = [lax.rem(op + j, N_OP) for j in range(1, N_OP)]

    barrier = pltpu.get_barrier_semaphore()
    for peer in peers:
        pl.semaphore_signal(barrier, inc=1, device_id=(peer, cell), device_id_type=MESH)
    for block in (prv, nxt):
        pl.semaphore_signal(barrier, inc=1, device_id=(op, block), device_id_type=MESH)
    pl.semaphore_wait(barrier, 5)

    coord_copies = []
    for j, peer in enumerate(peers):
        copy = pltpu.make_async_remote_copy(
            src_ref=coords_ref,
            dst_ref=cbuf.at[op],
            send_sem=c_send_sem.at[j],
            recv_sem=c_recv_sem.at[j],
            device_id=(peer, cell),
            device_id_type=MESH,
        )
        copy.start()
        coord_copies.append(copy)
    cbuf[op] = coords_ref[...]

    sub = lax.broadcasted_iota(jnp.int32, (8, LANES), 0)
    lane = lax.broadcasted_iota(jnp.int32, (8, LANES), 1)
    layer = lax.rem(sub, 4)
    first_op = sub < 4
    axial = lax.rem(lane, 4)
    stack[...] = jnp.zeros_like(stack)
    for a, ref in enumerate((start_ref, objective_ref, state_ref)):
        for p in range(OPS_HERE):
            for t in range(INST):
                stack[a * 10 + p * 5 + t, 0:VARS, :] = ref[p, t]
    stack[33, 0:6, :] = adjacency_ref[...].astype(jnp.float32)
    stack[34] = nodes_ref[...].astype(jnp.float32)

    def pick(p0, p1):
        return jnp.where(first_op, p0, p1)

    jac = [
        [[pick(jac_ref[0, d, u, v], jac_ref[1, d, u, v]) for v in range(VARS)] for u in range(VARS)]
        for d in range(3)
    ]
    damp = pick(damp_ref[0], damp_ref[1])
    freq = pick(freq_ref[0], freq_ref[1])

    for copy in coord_copies:
        copy.wait()

    for o in range(N_OP):
        for d in range(3):
            for h in range(2):
                nodebuf[d, 2 * o + h : 2 * o + h + 1, :] = cbuf[
                    o, d : d + 1, h * LANES : (h + 1) * LANES
                ]

    for tile in range(4):
        index = nodes_ref[:, tile * LANES : (tile + 1) * LANES]
        page = index // LANES
        within = lax.rem(index, LANES)
        for d in range(3):
            value = jnp.zeros((8, LANES), jnp.float32)
            for n in range(8):
                got = lanes_at(spread(nodebuf[d, n : n + 1, :]), within)
                value = jnp.where(page == n, got, value)
            stack[30 + d, :, tile * LANES : (tile + 1) * LANES] = value

    base = [jnp.floor(stack[30 + d, 0:1, :] + 0.5).astype(jnp.int32) for d in range(3)]
    pos = base[0] * LANES + base[1] * 4 + base[2]
    onehot = (
        (lax.broadcasted_iota(jnp.int32, (CELLS_HERE, CELLS_HERE), 0) == pos)
        .astype(jnp.float32)
        .astype(jnp.bfloat16)
    )
    moved = move_cells(stack[...].reshape(35 * 8, CELLS_HERE), onehot, 1).reshape(35, 8, CELLS_HERE)

    for a in range(3):
        for p in range(OPS_HERE):
            for t in range(INST):
                for l in range(4):
                    lattice[a, t, :, p * 4 + l, :] = moved[
                        a * 10 + p * 5 + t, 0:VARS, l * LANES : (l + 1) * LANES
                    ]
    for d in range(3):
        for l in range(4):
            part = moved[30 + d, :, l * LANES : (l + 1) * LANES]
            corner_lat[d, :, l, :] = part
            corner_lat[d, :, 4 + l, :] = part
    for l in range(4):
        part = moved[34, :, l * LANES : (l + 1) * LANES]
        slot_lat[:, l, :] = part

    def pos_of(cells):
        page = cells // LANES
        within = lax.rem(cells, LANES)
        value = jnp.zeros((8, LANES), jnp.int32)
        for n in range(4):
            got = lanes_at(spread(pos[:, n * LANES : (n + 1) * LANES]), within)
            value = jnp.where(page == n, got, value)
        return lax.rem(value, LANES)

    lower_map = pos_of(spread(send_ref[0:1, :]))
    upper_map = pos_of(spread(send_ref[1:2, :]))

    def pack(values, source):
        packed = []
        for g in range(GROUPS):
            total = values[4 * g]
            for r in range(1, 4):
                if 4 * g + r < STATE:
                    total = jnp.where(
                        layer == (source + r) % 4, pltpu.roll(values[4 * g + r], r, 0), total
                    )
            packed.append(total)
        return packed

    def exchange(number):
        used = pl.ds(0, GROUPS + 1 if number == 0 else GROUPS)
        up = pltpu.make_async_remote_copy(
            src_ref=up_send.at[number, used],
            dst_ref=low_recv.at[number, used],
            send_sem=up_send_sem.at[number],
            recv_sem=up_recv_sem.at[number],
            device_id=(op, nxt),
            device_id_type=MESH,
        )
        down = pltpu.make_async_remote_copy(
            src_ref=down_send.at[number, used],
            dst_ref=high_recv.at[number, used],
            send_sem=down_send_sem.at[number],
            recv_sem=down_recv_sem.at[number],
            device_id=(op, prv),
            device_id_type=MESH,
        )
        up.start()
        down.start()
        return up, down

    def fill(number, upward, downward):
        for g, value in enumerate(pack(upward, 3)):
            up_send[number, g] = value
        for g, value in enumerate(pack(downward, 0)):
            down_send[number, g] = value

    flow = [lattice[2, j // VARS, j % VARS] for j in range(STATE)]
    fill(0, flow, flow)
    up_send[0, GROUPS] = upper_map.astype(jnp.float32)
    down_send[0, GROUPS] = lower_map.astype(jnp.float32)
    copies = [exchange(0)]

    corner = [[corner_lat[d, c] for d in range(3)] for c in range(8)]
    center = [sum(corner[c][d] for c in range(8)) * 0.125 for d in range(3)]
    normals, areas, offsets = [], [], []
    volume = jnp.zeros((8, LANES), jnp.float32)
    for c0, c1, c2, c3 in FACE_CORNERS:
        first = [corner[c2][d] - corner[c0][d] for d in range(3)]
        second = [corner[c3][d] - corner[c1][d] for d in range(3)]
        normal = [0.5 * x for x in cross(first, second)]
        offset = [
            0.25 * (corner[c0][d] + corner[c1][d] + corner[c2][d] + corner[c3][d]) - center[d]
            for d in range(3)
        ]
        volume = volume + sum(offset[d] * normal[d] for d in range(3))
        normals.append(normal)
        offsets.append(offset)
        areas.append(jnp.sqrt(sum(normal[d] * normal[d] for d in range(3))))
    volume = volume * (1.0 / 3.0)
    area_sum = sum(areas)
    normal_total = [sum(normals[k][d] for k in range(6)) for d in range(3)]
    step = COURANT / ((1.0 + damp) * area_sum + 2.0 * freq * volume)

    inner = [None, None, lane >= 4, lane < LANES - 4, axial > 0, axial < 3]
    face_normal, face_area = [], []
    for k in range(6):
        keep = [0.5 * normals[k][d] for d in range(3)]
        area = 0.5 * damp * areas[k]
        if inner[k] is not None:
            keep = [jnp.where(inner[k], x, 0.0) for x in keep]
            area = jnp.where(inner[k], area, 0.0)
        face_normal.append(keep)
        face_area.append(area)
    half_total = [0.5 * normal_total[d] for d in range(3)]
    self_area = 0.5 * damp * area_sum
    freq_volume = freq * volume
    spectral = spectral_values()

    ghost_index = [None, None]

    def ghosts(number):
        low, high = [], []
        for g in range(GROUPS):
            from_low = lanes_at(low_recv[number, g], ghost_index[0])
            from_high = lanes_at(high_recv[number, g], ghost_index[1])
            for r in range(4):
                if 4 * g + r < STATE:
                    low.append(pltpu.roll(from_low, (8 - 3 - r) % 8, 0))
                    high.append(pltpu.roll(from_high, (3 - r) % 8, 0))
        return low, high

    for sweep in range(ITERS):
        adjoint = [lattice[0, j // VARS, j % VARS] for j in range(STATE)]
        upward, downward = [], []
        updates = []
        for t in range(INST):
            for v in range(VARS):
                j = t * VARS + v
                turned = [
                    sum(jac[d][u][v] * adjoint[t * VARS + u] for u in range(VARS)) for d in range(3)
                ]

                def outgoing(k):
                    return (
                        face_normal[k][0] * turned[0]
                        + face_normal[k][1] * turned[1]
                        + face_normal[k][2] * turned[2]
                        - face_area[k] * adjoint[j]
                    )

                upward.append(outgoing(1))
                downward.append(outgoing(0))
                update = (
                    half_total[0] * turned[0]
                    + half_total[1] * turned[1]
                    + half_total[2] * turned[2]
                    + self_area * adjoint[j]
                    + lattice[1, t, v]
                )
                mix = None
                for other in range(INST):
                    if other != t:
                        term = float(spectral[other, t]) * adjoint[other * VARS + v]
                        mix = term if mix is None else mix + term
                update = update + freq_volume * mix
                update = update + pltpu.roll(outgoing(3), 4, 1)
                update = update + pltpu.roll(outgoing(2), LANES - 4, 1)
                update = update + pltpu.roll(outgoing(5), 1, 1)
                update = update + pltpu.roll(outgoing(4), LANES - 1, 1)
                updates.append(update)
        fill(sweep + 1, upward, downward)
        copies.append(exchange(sweep + 1))
        if sweep == 0:
            for copy in copies[0]:
                copy.wait()
            for side in range(2):
                table = (low_recv, high_recv)[side][0, GROUPS].astype(jnp.int32)
                row = jnp.concatenate(
                    [
                        moved[33, side : side + 1, l * LANES : (l + 1) * LANES]
                        for l in ((0,) if side == 0 else (3,))
                    ],
                    axis=0,
                ).astype(jnp.int32)
                named = spread(row) - CELLS_HERE - side * LANES
                ghost_index[side] = lanes_at(table, jnp.clip(named, 0, LANES - 1))
        for copy in copies[sweep + 1]:
            copy.wait()
        low, high = ghosts(sweep + 1)
        for j in range(STATE):
            near_low = jnp.where(layer == 0, low[j], pltpu.roll(upward[j], 1, 0))
            near_high = jnp.where(layer == 3, high[j], pltpu.roll(downward[j], 7, 0))
            lattice[0, j // VARS, j % VARS] = adjoint[j] - step * (updates[j] + near_low + near_high)

    for p in range(OPS_HERE):
        for t in range(INST):
            for l in range(4):
                outbuf[p * 5 + t, 0:VARS, l * LANES : (l + 1) * LANES] = lattice[0, t, :, p * 4 + l, :]
            outbuf[p * 5 + t, VARS:8, :] = jnp.zeros((3, CELLS_HERE), jnp.float32)
    back = move_cells(outbuf[...].reshape(80, CELLS_HERE), onehot, 0).reshape(10, 8, CELLS_HERE)
    for p in range(OPS_HERE):
        for t in range(INST):
            out_ref[p, t] = back[p * 5 + t, 0:VARS, :]

    low, high = ghosts(0)
    along = [[None] * 3 for _ in range(6)]
    spread_sum = [None] * 6
    here = [None] * 3
    here_damp = None
    volume_sum = None

    def added(total, term):
        return term if total is None else total + term

    for t in range(INST):
        for v in range(VARS):
            j = t * VARS + v
            value = lattice[0, t, v]
            own = lattice[2, t, v]
            final = [
                sum(jac[d][u][v] * lattice[0, t, u] for u in range(VARS)) for d in range(3)
            ]
            mix = None
            for other in range(INST):
                if other != t:
                    mix = added(mix, float(spectral[t, other]) * lattice[2, other, v])
            volume_sum = added(volume_sum, value * mix)
            for d in range(3):
                here[d] = added(here[d], final[d] * own)
            here_damp = added(here_damp, value * own)
            far = [
                jnp.where(layer == 0, low[j], pltpu.roll(own, 1, 0)),
                jnp.where(layer == 3, high[j], pltpu.roll(own, 7, 0)),
                pltpu.roll(own, 4, 1),
                pltpu.roll(own, LANES - 4, 1),
                pltpu.roll(own, 1, 1),
                pltpu.roll(own, LANES - 1, 1),
            ]
            for k in range(6):
                for d in range(3):
                    along[k][d] = added(along[k][d], final[d] * far[k])
                spread_sum[k] = added(spread_sum[k], value * far[k])

    def both(x):
        return x + pltpu.roll(x, 4, 0)

    volume_grad = both(volume_sum * freq) * (WEIGHT / 3.0)
    cots = [[None] * 3 for _ in range(8)]
    center_cot = [-(0.125) * volume_grad * normal_total[d] for d in range(3)]
    for k, (c0, c1, c2, c3) in enumerate(FACE_CORNERS):
        far_along, far_damp = along[k], spread_sum[k]
        if inner[k] is not None:
            far_along = [jnp.where(inner[k], x, 0.0) for x in far_along]
            far_damp = jnp.where(inner[k], far_damp, 0.0)
        scale = both(damp * (here_damp - far_damp)) / areas[k]
        grad = [
            (0.5 * WEIGHT) * (both(here[d] + far_along[d]) + scale * normals[k][d])
            + volume_grad * offsets[k][d]
            for d in range(3)
        ]
        first = [corner[c2][d] - corner[c0][d] for d in range(3)]
        second = [corner[c3][d] - corner[c1][d] for d in range(3)]
        to_first = cross(second, grad)
        to_second = cross(grad, first)
        for d in range(3):
            middle = 0.25 * volume_grad * normals[k][d]
            cots[c0][d] = added(cots[c0][d], middle - 0.5 * to_first[d])
            cots[c2][d] = added(cots[c2][d], middle + 0.5 * to_first[d])
            cots[c1][d] = added(cots[c1][d], middle - 0.5 * to_second[d])
            cots[c3][d] = added(cots[c3][d], middle + 0.5 * to_second[d])
    cots = [[cots[c][d] + center_cot[d] for d in range(3)] for c in range(8)]

    def meet(bit, down, up, at_low, at_high):
        for c in range(8):
            if not c & bit:
                for d in range(3):
                    a, b = cots[c][d], cots[c | bit][d]
                    cots[c][d] = a + jnp.where(at_low, 0.0, down(b))
                    cots[c | bit][d] = b + jnp.where(at_high, 0.0, up(a))

    meet(1, lambda x: pltpu.roll(x, 1, 1), lambda x: pltpu.roll(x, LANES - 1, 1), axial == 0, axial == 3)
    meet(2, lambda x: pltpu.roll(x, 4, 1), lambda x: pltpu.roll(x, LANES - 4, 1), lane < 4, lane >= LANES - 4)
    meet(4, lambda x: pltpu.roll(x, 1, 0), lambda x: pltpu.roll(x, 7, 0), layer == 0, layer == 3)

    limits = (4, 32, 4)
    point = [
        jnp.clip(jnp.floor(jnp.clip(nodebuf[d], -1.0, 40.0) + 0.5).astype(jnp.int32), 0, limits[d])
        for d in range(3)
    ]
    home = [jnp.minimum(point[d], limits[d] - 1) for d in range(3)]
    source = ((point[0] - home[0]) * 4 + (point[1] - home[1]) * 2 + point[2] - home[2]) * 4 + home[0]
    within = home[1] * 4 + home[2]
    slot_number = sub * LANES + lane
    sens = [jnp.zeros((8, LANES), jnp.float32) for _ in range(3)]
    for c in range(8):
        slots = slot_lat[c]
        for l in range(4):
            name = lanes_at(spread(slots[l : l + 1]), within).astype(jnp.int32)
            chosen = jnp.logical_and(source == c * 4 + l, name == slot_number)
            for d in range(3):
                got = lanes_at(spread(cots[c][d][l : l + 1]), within)
                sens[d] = jnp.where(chosen, got, sens[d])

    rs_send[...] = jnp.zeros_like(rs_send)
    for o in range(N_OP):
        for d in range(3):
            rs_send[o, 2 * d : 2 * d + 2, :] = sens[d][2 * o : 2 * o + 2]
    sums = []
    for j, peer in enumerate(peers):
        copy = pltpu.make_async_remote_copy(
            src_ref=rs_send.at[peer],
            dst_ref=rs_recv.at[j],
            send_sem=r_send_sem.at[j],
            recv_sem=r_recv_sem.at[j],
            device_id=(peer, cell),
            device_id_type=MESH,
        )
        copy.start()
        sums.append(copy)
    total = rs_send[op]
    for j, copy in enumerate(sums):
        copy.wait()
        total = total + rs_recv[j]
    for d in range(3):
        for h in range(2):
            sens_ref[d : d + 1, h * LANES : (h + 1) * LANES] = total[2 * d + h : 2 * d + h + 1]


def per_device(
    flow_state,
    adjoint_start,
    objective_grad,
    adjacency,
    send_list,
    cell_nodes,
    coords,
    jacobians,
    dissipation,
    frequency,
):
    vmem = pl.BlockSpec(memory_space=pltpu.VMEM)
    smem = pl.BlockSpec(memory_space=pltpu.SMEM)
    f32 = jnp.float32
    dma = pltpu.SemaphoreType.DMA
    return pl.pallas_call(
        kernel,
        out_shape=(
            jax.ShapeDtypeStruct(flow_state.shape, f32),
            jax.ShapeDtypeStruct(coords.shape, f32),
        ),
        in_specs=[vmem] * 7 + [smem] * 3,
        out_specs=(vmem, vmem),
        scratch_shapes=[
            pltpu.VMEM((N_OP, 3, 256), f32),
            pltpu.VMEM((3, 8, LANES), f32),
            pltpu.VMEM((3, 8, CELLS_HERE), f32),
            pltpu.VMEM((35, 8, CELLS_HERE), f32),
            pltpu.VMEM((3, INST, VARS, 8, LANES), f32),
            pltpu.VMEM((3, 8, 8, LANES), f32),
            pltpu.VMEM((8, 8, LANES), f32),
            pltpu.VMEM((ITERS + 1, GROUPS + 1, 8, LANES), f32),
            pltpu.VMEM((ITERS + 1, GROUPS + 1, 8, LANES), f32),
            pltpu.VMEM((ITERS + 1, GROUPS + 1, 8, LANES), f32),
            pltpu.VMEM((ITERS + 1, GROUPS + 1, 8, LANES), f32),
            pltpu.VMEM((N_OP, 8, LANES), f32),
            pltpu.VMEM((N_OP - 1, 8, LANES), f32),
            pltpu.VMEM((10, 8, CELLS_HERE), f32),
            dma((3,)),
            dma((3,)),
            dma((3,)),
            dma((3,)),
            dma((ITERS + 1,)),
            dma((ITERS + 1,)),
            dma((ITERS + 1,)),
            dma((ITERS + 1,)),
        ],
        compiler_params=pltpu.CompilerParams(collective_id=0, has_side_effects=True),
    )(
        flow_state,
        adjoint_start,
        objective_grad,
        adjacency,
        send_list.reshape(2, LANES),
        cell_nodes,
        coords,
        jacobians,
        dissipation,
        frequency,
    )


def solution(mesh):
    in_specs = (
        P("op", None, None, "cell"),
        P("op", None, None, "cell"),
        P("op", None, None, "cell"),
        P(None, "cell"),
        P("cell"),
        P(None, "cell"),
        P(None, ("op", "cell")),
        P("op", None, None, None),
        P("op"),
        P("op"),
    )
    out_specs = (P("op", None, None, "cell"), P(None, ("op", "cell")))
    return jax.shard_map(
        per_device, mesh=mesh, in_specs=in_specs, out_specs=out_specs, check_vma=False
    )
```

profile of v0, /device:TPU:1, one launch (start us, length us, event | category | flops | bytes accessed | tf_op | source)
XLA Modules:
  0.0 58.2 jit_solution(10202592615919909508)
XLA Ops:
  0.6 1.3 %copy.15.jac_ref = f32[2,3,5,5]{3,2,1,0:T(8,128)} copy(f32[2,3,5,5]{3,0,2,1:T(2,128)} %param.17) | data formatting | bytes 1200 | tf_op args[7]
  2.0 0.0 copy-start
  2.0 1.6 %copy.12.state_ref = f32[2,5,5,512]{3,2,1,0:T(8,128)} copy(f32[2,5,5,512]{3,0,2,1:T(2,128)} %param.10) | data formatting | bytes 204800 | tf_op args[0]
  3.6 0.0 copy-done
  3.6 0.0 copy-start.1
  3.6 0.7 %copy.13.start_ref = f32[2,5,5,512]{3,2,1,0:T(8,128)} copy(f32[2,5,5,512]{3,0,2,1:T(2,128)S(1)} %copy-done) | data formatting | bytes 204800 | tf_op args[1]
  4.3 0.2 copy-done.1
  4.5 0.7 %copy.14.objective_ref = f32[2,5,5,512]{3,2,1,0:T(8,128)} copy(f32[2,5,5,512]{3,0,2,1:T(2,128)S(1)} %copy-done.1) | data formatting | bytes 204800 | tf_op args[2]
  5.2 50.8 %shard_map.113 = (f32[2,5,5,512]{3,2,1,0:T(8,128)}, f32[3,256]{1,0:T(4,128)}) custom-call(f32[2,5,5,512]{3,2,1,0:T(8,128)} %copy.12.state_ref, f32[2,5,5,512]{3,2,1,0:T(8,128)} %copy.13.start_ref, f32[2,5,5,512]{3,2,1,0:T(8,128)} %copy.14.objective_ref, s32[6,512]{1,0:T(8,128)} %adjacency_ref.1, s32[2,128]{1,0:T(2,128)} %bitcast.1, s32[8,512]{1,0:T(8,128)} %nodes_ref.1, ...), custom_call_target="tpu_custom_call" | custom-call | tf_op jit(solution)/shard_map/pallas_call | solution.py:517
  56.0 0.0 copy-start.2
  56.0 1.6 %copy.16 = f32[2,5,5,512]{3,0,2,1:T(2,128)} copy(f32[2,5,5,512]{3,2,1,0:T(8,128)} %get-tuple-element.2) | data formatting | bytes 204800 | tf_op jit(solution)/shard_map/pallas_call | solution.py:517
  57.6 0.0 copy-done.2
  57.6 0.6 %copy.18 = f32[3,256]{1,0:T(4,128)} copy(f32[3,256]{1,0:T(4,128)S(1)} %copy-done.2) | data formatting | bytes 6144
Async XLA Ops:
  2.0 1.6 %copy-start = (f32[2,5,5,512]{3,0,2,1:T(2,128)S(1)}, f32[2,5,5,512]{3,0,2,1:T(2,128)}, u32[]{:S(2)}) copy-start(f32[2,5,5,512]{3,0,2,1:T(2,128)} %param.11) | copy-start | bytes 307204
  3.6 0.9 %copy-start.1 = (f32[2,5,5,512]{3,0,2,1:T(2,128)S(1)}, f32[2,5,5,512]{3,0,2,1:T(2,128)}, u32[]{:S(2)}) copy-start(f32[2,5,5,512]{3,0,2,1:T(2,128)} %param.12) | copy-start | bytes 307204
  56.0 1.7 %copy-start.2 = (f32[3,256]{1,0:T(4,128)S(1)}, f32[3,256]{1,0:T(4,128)}, u32[]{:S(2)}) copy-start(f32[3,256]{1,0:T(4,128)} %get-tuple-element.7) | copy-start | bytes 9220
where the time goes:
time: 58.5 us; the launch traced here: 58.2 us
  Pallas kernels  50.8 us (87%)
  local copies, waits for them, and re-layouts  6.76 us (12%)
  between operations  0.65 us (1%)
    pallas_call x1, Pallas kernels, per_device(): pl.pallas_call(kernel, out_shape=(jax.ShapeDtypeStruct(flow_state.shape,...  50.8 us
    unnamed x11, local copies, waits for them, and re-layouts  5.12 us
    pallas_call x1, local copies, waits for them, and re-layouts, per_device(): pl.pallas_call(kernel, out_shape=(jax.ShapeDtypeStruct(flow_state.shape,...  1.64 us

commit v1 on v0

--- a/solution.py
+++ b/solution.py
@@ -62,6 +62,18 @@
 
 
 def kernel(
+    state_in,
+    start_in,
+    objective_in,
+    adjacency_in,
+    send_in,
+    nodes_in,
+    coords_in,
+    jac_in,
+    damp_in,
+    freq_in,
+    out_hbm,
+    sens_ref,
     state_ref,
     start_ref,
     objective_ref,
@@ -73,11 +85,10 @@
     damp_ref,
     freq_ref,
     out_ref,
-    sens_ref,
     cbuf,
     nodebuf,
-    cornerbuf,
     stack,
+    stack_late,
     lattice,
     corner_lat,
     slot_lat,
@@ -88,6 +99,8 @@
     rs_send,
     rs_recv,
     outbuf,
+    fetch_sem,
+    out_sem,
     c_send_sem,
     c_recv_sem,
     r_send_sem,
@@ -104,12 +117,31 @@
     prv = lax.rem(cell + n_cell - 1, n_cell)
     peers = [lax.rem(op + j, N_OP) for j in range(1, N_OP)]
 
+    fetches = []
+    pairs = (
+        (coords_in, coords_ref),
+        (nodes_in, nodes_ref),
+        (adjacency_in, adjacency_ref),
+        (send_in, send_ref),
+        (start_in, start_ref),
+        (jac_in, jac_ref),
+        (damp_in, damp_ref),
+        (freq_in, freq_ref),
+        (objective_in, objective_ref),
+        (state_in, state_ref),
+    )
+    for j, (source, target) in enumerate(pairs):
+        fetch = pltpu.make_async_copy(source, target, fetch_sem.at[j])
+        fetch.start()
+        fetches.append(fetch)
+
     barrier = pltpu.get_barrier_semaphore()
     for peer in peers:
         pl.semaphore_signal(barrier, inc=1, device_id=(peer, cell), device_id_type=MESH)
     for block in (prv, nxt):
         pl.semaphore_signal(barrier, inc=1, device_id=(op, block), device_id_type=MESH)
     pl.semaphore_wait(barrier, 5)
+    fetches[0].wait()
 
     coord_copies = []
     for j, peer in enumerate(peers):
@@ -127,22 +159,26 @@
 
     sub = lax.broadcasted_iota(jnp.int32, (8, LANES), 0)
     lane = lax.broadcasted_iota(jnp.int32, (8, LANES), 1)
-    layer = lax.rem(sub, 4)
-    first_op = sub < 4
+    layer = sub // 2
+    first_op = lax.rem(sub, 2) == 0
     axial = lax.rem(lane, 4)
-    stack[...] = jnp.zeros_like(stack)
-    for a, ref in enumerate((start_ref, objective_ref, state_ref)):
-        for p in range(OPS_HERE):
-            for t in range(INST):
-                stack[a * 10 + p * 5 + t, 0:VARS, :] = ref[p, t]
-    stack[33, 0:6, :] = adjacency_ref[...].astype(jnp.float32)
-    stack[34] = nodes_ref[...].astype(jnp.float32)
+    for fetch in fetches[1:]:
+        fetch.wait()
+    stack[48:56, :] = jnp.zeros((8, CELLS_HERE), jnp.float32)
+    stack[80:88, :] = jnp.zeros((8, CELLS_HERE), jnp.float32)
+    stack_late[96:104, :] = jnp.zeros((8, CELLS_HERE), jnp.float32)
+    for j in range(STATE):
+        stack[2 * j : 2 * j + 2, :] = start_ref[j]
+        stack_late[2 * j : 2 * j + 2, :] = objective_ref[j]
+        stack_late[50 + 2 * j : 52 + 2 * j, :] = state_ref[j]
+    stack[80:86, :] = adjacency_ref[...].astype(jnp.float32)
+    stack[88:96, :] = nodes_ref[...].astype(jnp.float32)
 
     def pick(p0, p1):
         return jnp.where(first_op, p0, p1)
 
     jac = [
-        [[pick(jac_ref[0, d, u, v], jac_ref[1, d, u, v]) for v in range(VARS)] for u in range(VARS)]
+        [[pick(jac_ref[d, u, 0, v], jac_ref[d, u, 1, v]) for v in range(VARS)] for u in range(VARS)]
         for d in range(3)
     ]
     damp = pick(damp_ref[0], damp_ref[1])
@@ -167,32 +203,32 @@
             for n in range(8):
                 got = lanes_at(spread(nodebuf[d, n : n + 1, :]), within)
                 value = jnp.where(page == n, got, value)
-            stack[30 + d, :, tile * LANES : (tile + 1) * LANES] = value
-
-    base = [jnp.floor(stack[30 + d, 0:1, :] + 0.5).astype(jnp.int32) for d in range(3)]
+            stack[56 + 8 * d : 64 + 8 * d, tile * LANES : (tile + 1) * LANES] = value
+
+    base = [jnp.floor(stack[56 + 8 * d : 57 + 8 * d, :] + 0.5).astype(jnp.int32) for d in range(3)]
     pos = base[0] * LANES + base[1] * 4 + base[2]
     onehot = (
         (lax.broadcasted_iota(jnp.int32, (CELLS_HERE, CELLS_HERE), 0) == pos)
         .astype(jnp.float32)
         .astype(jnp.bfloat16)
     )
-    moved = move_cells(stack[...].reshape(35 * 8, CELLS_HERE), onehot, 1).reshape(35, 8, CELLS_HERE)
-
-    for a in range(3):
-        for p in range(OPS_HERE):
-            for t in range(INST):
-                for l in range(4):
-                    lattice[a, t, :, p * 4 + l, :] = moved[
-                        a * 10 + p * 5 + t, 0:VARS, l * LANES : (l + 1) * LANES
-                    ]
-    for d in range(3):
-        for l in range(4):
-            part = moved[30 + d, :, l * LANES : (l + 1) * LANES]
-            corner_lat[d, :, l, :] = part
-            corner_lat[d, :, 4 + l, :] = part
+    moved = move_cells(stack[...], onehot, 1)
+
+    def to_lattice(array, rows, base_row):
+        for j in range(STATE):
+            row = base_row + 2 * j
+            for l in range(4):
+                lattice[array, j, 2 * l : 2 * l + 2, :] = rows[
+                    row : row + 2, l * LANES : (l + 1) * LANES
+                ]
+
+    to_lattice(0, moved, 0)
     for l in range(4):
-        part = moved[34, :, l * LANES : (l + 1) * LANES]
-        slot_lat[:, l, :] = part
+        for d in range(3):
+            part = moved[56 + 8 * d : 64 + 8 * d, l * LANES : (l + 1) * LANES]
+            corner_lat[d, :, 2 * l, :] = part
+            corner_lat[d, :, 2 * l + 1, :] = part
+        slot_lat[:, l, :] = moved[88:96, l * LANES : (l + 1) * LANES]
 
     def pos_of(cells):
         page = cells // LANES
@@ -213,7 +249,7 @@
             for r in range(1, 4):
                 if 4 * g + r < STATE:
                     total = jnp.where(
-                        layer == (source + r) % 4, pltpu.roll(values[4 * g + r], r, 0), total
+                        layer == (source + r) % 4, pltpu.roll(values[4 * g + r], 2 * r, 0), total
                     )
             packed.append(total)
         return packed
@@ -246,11 +282,8 @@
         for g, value in enumerate(pack(downward, 0)):
             down_send[number, g] = value
 
-    flow = [lattice[2, j // VARS, j % VARS] for j in range(STATE)]
-    fill(0, flow, flow)
     up_send[0, GROUPS] = upper_map.astype(jnp.float32)
     down_send[0, GROUPS] = lower_map.astype(jnp.float32)
-    copies = [exchange(0)]
 
     corner = [[corner_lat[d, c] for d in range(3)] for c in range(8)]
     center = [sum(corner[c][d] for c in range(8)) * 0.125 for d in range(3)]
@@ -297,84 +330,86 @@
             from_high = lanes_at(high_recv[number, g], ghost_index[1])
             for r in range(4):
                 if 4 * g + r < STATE:
-                    low.append(pltpu.roll(from_low, (8 - 3 - r) % 8, 0))
-                    high.append(pltpu.roll(from_high, (3 - r) % 8, 0))
+                    low.append(pltpu.roll(from_low, (2 - 2 * r) % 8, 0))
+                    high.append(pltpu.roll(from_high, (6 - 2 * r) % 8, 0))
         return low, high
 
+    def turn(values):
+        return [
+            [
+                sum(jac[d][u][v] * values[t * VARS + u] for u in range(VARS))
+                for t in range(INST)
+                for v in range(VARS)
+            ]
+            for d in range(3)
+        ]
+
+    adjoint = [lattice[0, j] for j in range(STATE)]
     for sweep in range(ITERS):
-        adjoint = [lattice[0, j // VARS, j % VARS] for j in range(STATE)]
-        upward, downward = [], []
+        turned = turn(adjoint)
+
+        def outgoing(k, j):
+            return (
+                face_normal[k][0] * turned[0][j]
+                + face_normal[k][1] * turned[1][j]
+                + face_normal[k][2] * turned[2][j]
+                - face_area[k] * adjoint[j]
+            )
+
+        upward = [outgoing(1, j) for j in range(STATE)]
+        downward = [outgoing(0, j) for j in range(STATE)]
+        fill(sweep, upward, downward)
+        pair = exchange(sweep)
+        if sweep == 0:
+            moved_late = move_cells(stack_late[...], onehot, 1)
+            to_lattice(1, moved_late, 0)
+            to_lattice(2, moved_late, 50)
+            flow = [lattice[2, j] for j in range(STATE)]
+            fill(ITERS, flow, flow)
+            flow_pair = exchange(ITERS)
         updates = []
-        for t in range(INST):
-            for v in range(VARS):
-                j = t * VARS + v
-                turned = [
-                    sum(jac[d][u][v] * adjoint[t * VARS + u] for u in range(VARS)) for d in range(3)
-                ]
-
-                def outgoing(k):
-                    return (
-                        face_normal[k][0] * turned[0]
-                        + face_normal[k][1] * turned[1]
-                        + face_normal[k][2] * turned[2]
-                        - face_area[k] * adjoint[j]
-                    )
-
-                upward.append(outgoing(1))
-                downward.append(outgoing(0))
-                update = (
-                    half_total[0] * turned[0]
-                    + half_total[1] * turned[1]
-                    + half_total[2] * turned[2]
-                    + self_area * adjoint[j]
-                    + lattice[1, t, v]
-                )
-                mix = None
-                for other in range(INST):
-                    if other != t:
-                        term = float(spectral[other, t]) * adjoint[other * VARS + v]
-                        mix = term if mix is None else mix + term
-                update = update + freq_volume * mix
-                update = update + pltpu.roll(outgoing(3), 4, 1)
-                update = update + pltpu.roll(outgoing(2), LANES - 4, 1)
-                update = update + pltpu.roll(outgoing(5), 1, 1)
-                update = update + pltpu.roll(outgoing(4), LANES - 1, 1)
-                updates.append(update)
-        fill(sweep + 1, upward, downward)
-        copies.append(exchange(sweep + 1))
+        for j in range(STATE):
+            t, v = j // VARS, j % VARS
+            update = (
+                half_total[0] * turned[0][j]
+                + half_total[1] * turned[1][j]
+                + half_total[2] * turned[2][j]
+                + self_area * adjoint[j]
+                + lattice[1, j]
+            )
+            mix = None
+            for other in range(INST):
+                if other != t:
+                    term = float(spectral[other, t]) * adjoint[other * VARS + v]
+                    mix = term if mix is None else mix + term
+            update = update + freq_volume * mix
+            update = update + pltpu.roll(outgoing(3, j), 4, 1)
+            update = update + pltpu.roll(outgoing(2, j), LANES - 4, 1)
+            update = update + pltpu.roll(outgoing(5, j), 1, 1)
+            update = update + pltpu.roll(outgoing(4, j), LANES - 1, 1)
+            update = update + jnp.where(layer == 0, 0.0, pltpu.roll(upward[j], 2, 0))
+            update = update + jnp.where(layer == 3, 0.0, pltpu.roll(downward[j], 6, 0))
+            updates.append(adjoint[j] - step * update)
+        for copy in pair:
+            copy.wait()
         if sweep == 0:
-            for copy in copies[0]:
-                copy.wait()
             for side in range(2):
                 table = (low_recv, high_recv)[side][0, GROUPS].astype(jnp.int32)
-                row = jnp.concatenate(
-                    [
-                        moved[33, side : side + 1, l * LANES : (l + 1) * LANES]
-                        for l in ((0,) if side == 0 else (3,))
-                    ],
-                    axis=0,
-                ).astype(jnp.int32)
-                named = spread(row) - CELLS_HERE - side * LANES
+                tile = 3 * side
+                row = moved[80 + side : 81 + side, tile * LANES : (tile + 1) * LANES]
+                named = spread(row.astype(jnp.int32)) - CELLS_HERE - side * LANES
                 ghost_index[side] = lanes_at(table, jnp.clip(named, 0, LANES - 1))
-        for copy in copies[sweep + 1]:
-            copy.wait()
-        low, high = ghosts(sweep + 1)
-        for j in range(STATE):
-            near_low = jnp.where(layer == 0, low[j], pltpu.roll(upward[j], 1, 0))
-            near_high = jnp.where(layer == 3, high[j], pltpu.roll(downward[j], 7, 0))
-            lattice[0, j // VARS, j % VARS] = adjoint[j] - step * (updates[j] + near_low + near_high)
-
-    for p in range(OPS_HERE):
-        for t in range(INST):
-            for l in range(4):
-                outbuf[p * 5 + t, 0:VARS, l * LANES : (l + 1) * LANES] = lattice[0, t, :, p * 4 + l, :]
-            outbuf[p * 5 + t, VARS:8, :] = jnp.zeros((3, CELLS_HERE), jnp.float32)
-    back = move_cells(outbuf[...].reshape(80, CELLS_HERE), onehot, 0).reshape(10, 8, CELLS_HERE)
-    for p in range(OPS_HERE):
-        for t in range(INST):
-            out_ref[p, t] = back[p * 5 + t, 0:VARS, :]
-
-    low, high = ghosts(0)
+        low, high = ghosts(sweep)
+        adjoint = [
+            updates[j] - step * jnp.where(layer == 0, low[j], jnp.where(layer == 3, high[j], 0.0))
+            for j in range(STATE)
+        ]
+
+    for copy in flow_pair:
+        copy.wait()
+
+    low, high = ghosts(ITERS)
+    final_rows = turn(adjoint)
     along = [[None] * 3 for _ in range(6)]
     spread_sum = [None] * 6
     here = [None] * 3
@@ -387,22 +422,20 @@
     for t in range(INST):
         for v in range(VARS):
             j = t * VARS + v
-            value = lattice[0, t, v]
-            own = lattice[2, t, v]
-            final = [
-                sum(jac[d][u][v] * lattice[0, t, u] for u in range(VARS)) for d in range(3)
-            ]
+            value = adjoint[j]
+            own = lattice[2, j]
+            final = [final_rows[d][j] for d in range(3)]
             mix = None
             for other in range(INST):
                 if other != t:
-                    mix = added(mix, float(spectral[t, other]) * lattice[2, other, v])
+                    mix = added(mix, float(spectral[t, other]) * lattice[2, other * VARS + v])
             volume_sum = added(volume_sum, value * mix)
             for d in range(3):
                 here[d] = added(here[d], final[d] * own)
             here_damp = added(here_damp, value * own)
             far = [
-                jnp.where(layer == 0, low[j], pltpu.roll(own, 1, 0)),
-                jnp.where(layer == 3, high[j], pltpu.roll(own, 7, 0)),
+                jnp.where(layer == 0, low[j], pltpu.roll(own, 2, 0)),
+                jnp.where(layer == 3, high[j], pltpu.roll(own, 6, 0)),
                 pltpu.roll(own, 4, 1),
                 pltpu.roll(own, LANES - 4, 1),
                 pltpu.roll(own, 1, 1),
@@ -414,7 +447,7 @@
                 spread_sum[k] = added(spread_sum[k], value * far[k])
 
     def both(x):
-        return x + pltpu.roll(x, 4, 0)
+        return x + jnp.where(first_op, pltpu.roll(x, 7, 0), pltpu.roll(x, 1, 0))
 
     volume_grad = both(volume_sum * freq) * (WEIGHT / 3.0)
     cots = [[None] * 3 for _ in range(8)]
@@ -452,7 +485,7 @@
 
     meet(1, lambda x: pltpu.roll(x, 1, 1), lambda x: pltpu.roll(x, LANES - 1, 1), axial == 0, axial == 3)
     meet(2, lambda x: pltpu.roll(x, 4, 1), lambda x: pltpu.roll(x, LANES - 4, 1), lane < 4, lane >= LANES - 4)
-    meet(4, lambda x: pltpu.roll(x, 1, 0), lambda x: pltpu.roll(x, 7, 0), layer == 0, layer == 3)
+    meet(4, lambda x: pltpu.roll(x, 2, 0), lambda x: pltpu.roll(x, 6, 0), layer == 0, layer == 3)
 
     limits = (4, 32, 4)
     point = [
@@ -470,7 +503,7 @@
             name = lanes_at(spread(slots[l : l + 1]), within).astype(jnp.int32)
             chosen = jnp.logical_and(source == c * 4 + l, name == slot_number)
             for d in range(3):
-                got = lanes_at(spread(cots[c][d][l : l + 1]), within)
+                got = lanes_at(spread(cots[c][d][2 * l : 2 * l + 1]), within)
                 sens[d] = jnp.where(chosen, got, sens[d])
 
     rs_send[...] = jnp.zeros_like(rs_send)
@@ -489,6 +522,17 @@
         )
         copy.start()
         sums.append(copy)
+
+    outbuf[48:56, :] = jnp.zeros((8, CELLS_HERE), jnp.float32)
+    for j in range(STATE):
+        for l in range(4):
+            outbuf[2 * j : 2 * j + 2, l * LANES : (l + 1) * LANES] = adjoint[j][2 * l : 2 * l + 2]
+    back = move_cells(outbuf[...], onehot, 0)
+    for j in range(STATE):
+        out_ref[j] = back[2 * j : 2 * j + 2]
+    put = pltpu.make_async_copy(out_ref, out_hbm, out_sem)
+    put.start()
+
     total = rs_send[op]
     for j, copy in enumerate(sums):
         copy.wait()
@@ -496,6 +540,7 @@
     for d in range(3):
         for h in range(2):
             sens_ref[d : d + 1, h * LANES : (h + 1) * LANES] = total[2 * d + h : 2 * d + h + 1]
+    put.wait()
 
 
 def per_device(
@@ -510,33 +555,51 @@
     dissipation,
     frequency,
 ):
-    vmem = pl.BlockSpec(memory_space=pltpu.VMEM)
-    smem = pl.BlockSpec(memory_space=pltpu.SMEM)
-    f32 = jnp.float32
+    anywhere = pl.BlockSpec(memory_space=pl.ANY)
+    f32, i32 = jnp.float32, jnp.int32
     dma = pltpu.SemaphoreType.DMA
-    return pl.pallas_call(
+
+    def pairs(x):
+        return x.transpose(1, 2, 0, 3).reshape(STATE, OPS_HERE, CELLS_HERE)
+
+    rows = pltpu.VMEM((STATE, OPS_HERE, CELLS_HERE), f32)
+    message = pltpu.VMEM((ITERS + 1, GROUPS + 1, 8, LANES), f32)
+    adjoint, sens = pl.pallas_call(
         kernel,
         out_shape=(
-            jax.ShapeDtypeStruct(flow_state.shape, f32),
+            jax.ShapeDtypeStruct((STATE, OPS_HERE, CELLS_HERE), f32),
             jax.ShapeDtypeStruct(coords.shape, f32),
         ),
-        in_specs=[vmem] * 7 + [smem] * 3,
-        out_specs=(vmem, vmem),
+        in_specs=[anywhere] * 10,
+        out_specs=(anywhere, pl.BlockSpec(memory_space=pltpu.VMEM)),
         scratch_shapes=[
+            rows,
+            rows,
+            rows,
+            pltpu.VMEM((6, CELLS_HERE), i32),
+            pltpu.VMEM((2, LANES), i32),
+            pltpu.VMEM((8, CELLS_HERE), i32),
+            pltpu.VMEM((3, 256), f32),
+            pltpu.SMEM((3, VARS, OPS_HERE, VARS), f32),
+            pltpu.SMEM((OPS_HERE,), f32),
+            pltpu.SMEM((OPS_HERE,), f32),
+            rows,
             pltpu.VMEM((N_OP, 3, 256), f32),
             pltpu.VMEM((3, 8, LANES), f32),
-            pltpu.VMEM((3, 8, CELLS_HERE), f32),
-            pltpu.VMEM((35, 8, CELLS_HERE), f32),
-            pltpu.VMEM((3, INST, VARS, 8, LANES), f32),
+            pltpu.VMEM((96, CELLS_HERE), f32),
+            pltpu.VMEM((104, CELLS_HERE), f32),
+            pltpu.VMEM((3, STATE, 8, LANES), f32),
             pltpu.VMEM((3, 8, 8, LANES), f32),
             pltpu.VMEM((8, 8, LANES), f32),
-            pltpu.VMEM((ITERS + 1, GROUPS + 1, 8, LANES), f32),
-            pltpu.VMEM((ITERS + 1, GROUPS + 1, 8, LANES), f32),
-            pltpu.VMEM((ITERS + 1, GROUPS + 1, 8, LANES), f32),
-            pltpu.VMEM((ITERS + 1, GROUPS + 1, 8, LANES), f32),
+            message,
+            message,
+            message,
+            message,
             pltpu.VMEM((N_OP, 8, LANES), f32),
             pltpu.VMEM((N_OP - 1, 8, LANES), f32),
-            pltpu.VMEM((10, 8, CELLS_HERE), f32),
+            pltpu.VMEM((56, CELLS_HERE), f32),
+            dma((10,)),
+            dma,
             dma((3,)),
             dma((3,)),
             dma((3,)),
@@ -548,17 +611,19 @@
         ],
         compiler_params=pltpu.CompilerParams(collective_id=0, has_side_effects=True),
     )(
-        flow_state,
-        adjoint_start,
-        objective_grad,
+        pairs(flow_state),
+        pairs(adjoint_start),
+        pairs(objective_grad),
         adjacency,
         send_list.reshape(2, LANES),
         cell_nodes,
         coords,
-        jacobians,
+        jacobians.transpose(1, 2, 0, 3),
         dissipation,
         frequency,
     )
+    adjoint = adjoint.reshape(INST, VARS, OPS_HERE, CELLS_HERE).transpose(2, 0, 1, 3)
+    return adjoint, sens
 
 
 def solution(mesh):

time: 58.5 us -> 51.8 us (0.89)
  local copies, waits for them, and re-layouts: 6.76 us -> 2.14 us
  Pallas kernels: 50.8 us -> 48.9 us
    unnamed x11 -> x4, local copies, waits for them, and re-layouts: 5.12 us -> 2.14 us
    pallas_call x1, Pallas kernels: 50.8 us -> 48.9 us  [per_device(): pl.pallas_call(kernel, out_shape=(jax.ShapeDtypeStruct((STATE, OPS_HERE,...]
    pallas_call x1 -> x0, local copies, waits for them, and re-layouts: 1.64 us -> none  [per_device(): pl.pallas_call(kernel, out_shape=(jax.ShapeDtypeStruct(flow_state.shape,...]
where the time goes in v1:
time: 51.8 us; the launch traced here: 51.7 us
  Pallas kernels  48.9 us (94%)
  local copies, waits for them, and re-layouts  2.14 us (4%)
  between operations  0.65 us (1%)
    pallas_call x1, Pallas kernels, per_device(): pl.pallas_call(kernel, out_shape=(jax.ShapeDtypeStruct((STATE, OPS_HERE,...  48.9 us
    unnamed x4, local copies, waits for them, and re-layouts  2.14 us

profile of v1, /device:TPU:1, one launch (start us, length us, event | category | flops | bytes accessed | tf_op | source)
XLA Modules:
  0.0 51.7 jit_solution(757806379162900090)
XLA Ops:
  0.6 48.9 %shard_map.113 = (f32[25,2,512]{2,1,0:T(2,128)}, f32[3,256]{1,0:T(4,128)}) custom-call(f32[25,2,512]{2,1,0:T(2,128)} %bitcast.14, f32[25,2,512]{2,1,0:T(2,128)} %bitcast.15, f32[25,2,512]{2,1,0:T(2,128)} %bitcast.16, s32[6,512]{1,0:T(8,128)} %adjacency_in.1, s32[2,128]{1,0:T(2,128)} %bitcast.19, s32[8,512]{1,0:T(8,128)} %nodes_in.1, f32[3,256]{1,0:T(4,128)} %coords_in.1, ...), custom_call_target="tpu_custom_call" | custom-call | tf_op jit(solution)/shard_map/pallas_call | solution.py:567
  49.5 0.0 copy-start
  49.5 1.5 %copy.14 = f32[2,5,5,512]{3,0,2,1:T(2,128)} copy(f32[2,5,5,512]{3,0,2,1:T(2,128)} %bitcast.17) | data formatting | bytes 204800
  51.1 0.0 copy-done
  51.1 0.6 %copy.15 = f32[3,256]{1,0:T(4,128)} copy(f32[3,256]{1,0:T(4,128)S(1)} %copy-done) | data formatting | bytes 6144
Async XLA Ops:
  49.5 1.6 %copy-start = (f32[3,256]{1,0:T(4,128)S(1)}, f32[3,256]{1,0:T(4,128)}, u32[]{:S(2)}) copy-start(f32[3,256]{1,0:T(4,128)} %get-tuple-element.9) | copy-start | bytes 9220

commit v2 on v1

--- a/solution.py
+++ b/solution.py
@@ -96,6 +96,14 @@
     down_send,
     low_recv,
     high_recv,
+    map_up,
+    map_down,
+    map_low,
+    map_high,
+    low_state,
+    high_state,
+    low_corner,
+    high_corner,
     rs_send,
     rs_recv,
     outbuf,
@@ -254,19 +262,18 @@
             packed.append(total)
         return packed
 
-    def exchange(number):
-        used = pl.ds(0, GROUPS + 1 if number == 0 else GROUPS)
+    def exchange(number, up_from, low_to, down_from, high_to):
         up = pltpu.make_async_remote_copy(
-            src_ref=up_send.at[number, used],
-            dst_ref=low_recv.at[number, used],
+            src_ref=up_from,
+            dst_ref=low_to,
             send_sem=up_send_sem.at[number],
             recv_sem=up_recv_sem.at[number],
             device_id=(op, nxt),
             device_id_type=MESH,
         )
         down = pltpu.make_async_remote_copy(
-            src_ref=down_send.at[number, used],
-            dst_ref=high_recv.at[number, used],
+            src_ref=down_from,
+            dst_ref=high_to,
             send_sem=down_send_sem.at[number],
             recv_sem=down_recv_sem.at[number],
             device_id=(op, prv),
@@ -274,60 +281,79 @@
         )
         up.start()
         down.start()
-        return up, down
-
-    def fill(number, upward, downward):
-        for g, value in enumerate(pack(upward, 3)):
-            up_send[number, g] = value
-        for g, value in enumerate(pack(downward, 0)):
-            down_send[number, g] = value
-
-    up_send[0, GROUPS] = upper_map.astype(jnp.float32)
-    down_send[0, GROUPS] = lower_map.astype(jnp.float32)
-
-    corner = [[corner_lat[d, c] for d in range(3)] for c in range(8)]
-    center = [sum(corner[c][d] for c in range(8)) * 0.125 for d in range(3)]
-    normals, areas, offsets = [], [], []
-    volume = jnp.zeros((8, LANES), jnp.float32)
-    for c0, c1, c2, c3 in FACE_CORNERS:
-        first = [corner[c2][d] - corner[c0][d] for d in range(3)]
-        second = [corner[c3][d] - corner[c1][d] for d in range(3)]
-        normal = [0.5 * x for x in cross(first, second)]
-        offset = [
-            0.25 * (corner[c0][d] + corner[c1][d] + corner[c2][d] + corner[c3][d]) - center[d]
-            for d in range(3)
-        ]
-        volume = volume + sum(offset[d] * normal[d] for d in range(3))
-        normals.append(normal)
-        offsets.append(offset)
-        areas.append(jnp.sqrt(sum(normal[d] * normal[d] for d in range(3))))
-    volume = volume * (1.0 / 3.0)
-    area_sum = sum(areas)
-    normal_total = [sum(normals[k][d] for k in range(6)) for d in range(3)]
-    step = COURANT / ((1.0 + damp) * area_sum + 2.0 * freq * volume)
+        copies.extend((up, down))
+
+    copies = []
+
+    def end_names(side):
+        tile = 3 * side
+        row = moved[80 + side : 81 + side, tile * LANES : (tile + 1) * LANES]
+        named = spread(row.astype(jnp.int32)) - CELLS_HERE - side * LANES
+        return jnp.clip(named, 0, LANES - 1)
+
+    low_names, high_names = end_names(0), end_names(1)
+    map_up[0] = upper_map.astype(jnp.float32)
+    map_up[1] = high_names.astype(jnp.float32)
+    map_down[0] = lower_map.astype(jnp.float32)
+    map_down[1] = low_names.astype(jnp.float32)
+    exchange(0, lattice.at[0], low_state.at[0], lattice.at[0], high_state.at[0])
+    exchange(1, corner_lat, low_corner, corner_lat, high_corner)
+    exchange(2, map_up, map_low, map_down, map_high)
+    moved_late = move_cells(stack_late[...], onehot, 1)
+    to_lattice(1, moved_late, 0)
+    exchange(3, lattice.at[1], low_state.at[1], lattice.at[1], high_state.at[1])
+    to_lattice(2, moved_late, 50)
+    flow = [lattice[2, j] for j in range(STATE)]
+    for g, value in enumerate(pack(flow, 3)):
+        up_send[g] = value
+    for g, value in enumerate(pack(flow, 0)):
+        down_send[g] = value
+    exchange(4, up_send, low_recv, down_send, high_recv)
 
     inner = [None, None, lane >= 4, lane < LANES - 4, axial > 0, axial < 3]
-    face_normal, face_area = [], []
-    for k in range(6):
-        keep = [0.5 * normals[k][d] for d in range(3)]
-        area = 0.5 * damp * areas[k]
-        if inner[k] is not None:
-            keep = [jnp.where(inner[k], x, 0.0) for x in keep]
-            area = jnp.where(inner[k], area, 0.0)
-        face_normal.append(keep)
-        face_area.append(area)
-    half_total = [0.5 * normal_total[d] for d in range(3)]
-    self_area = 0.5 * damp * area_sum
-    freq_volume = freq * volume
+
+    def geometry(points):
+        corner = [[points[d, c] for d in range(3)] for c in range(8)]
+        center = [sum(corner[c][d] for c in range(8)) * 0.125 for d in range(3)]
+        normals, areas, offsets = [], [], []
+        volume = jnp.zeros((8, LANES), jnp.float32)
+        for c0, c1, c2, c3 in FACE_CORNERS:
+            first = [corner[c2][d] - corner[c0][d] for d in range(3)]
+            second = [corner[c3][d] - corner[c1][d] for d in range(3)]
+            normal = [0.5 * x for x in cross(first, second)]
+            offset = [
+                0.25 * (corner[c0][d] + corner[c1][d] + corner[c2][d] + corner[c3][d]) - center[d]
+                for d in range(3)
+            ]
+            volume = volume + sum(offset[d] * normal[d] for d in range(3))
+            normals.append(normal)
+            offsets.append(offset)
+            areas.append(jnp.sqrt(sum(normal[d] * normal[d] for d in range(3))))
+        volume = volume * (1.0 / 3.0)
+        area_sum = sum(areas)
+        normal_total = [sum(normals[k][d] for k in range(6)) for d in range(3)]
+        step = COURANT / ((1.0 + damp) * area_sum + 2.0 * freq * volume)
+        face_normal, face_area = [], []
+        for k in range(6):
+            keep = [0.5 * normals[k][d] for d in range(3)]
+            area = 0.5 * damp * areas[k]
+            if inner[k] is not None:
+                keep = [jnp.where(inner[k], x, 0.0) for x in keep]
+                area = jnp.where(inner[k], area, 0.0)
+            face_normal.append(keep)
+            face_area.append(area)
+        half_total = [0.5 * normal_total[d] for d in range(3)]
+        sweep_terms = (face_normal, face_area, half_total, 0.5 * damp * area_sum, freq * volume, step)
+        return sweep_terms, (corner, normals, areas, offsets, normal_total)
+
+    own_terms, (corner, normals, areas, offsets, normal_total) = geometry(corner_lat)
     spectral = spectral_values()
 
-    ghost_index = [None, None]
-
-    def ghosts(number):
+    def ghosts():
         low, high = [], []
         for g in range(GROUPS):
-            from_low = lanes_at(low_recv[number, g], ghost_index[0])
-            from_high = lanes_at(high_recv[number, g], ghost_index[1])
+            from_low = lanes_at(low_recv[g], ghost_index[0])
+            from_high = lanes_at(high_recv[g], ghost_index[1])
             for r in range(4):
                 if 4 * g + r < STATE:
                     low.append(pltpu.roll(from_low, (2 - 2 * r) % 8, 0))
@@ -344,71 +370,93 @@
             for d in range(3)
         ]
 
+    for copy in copies:
+        copy.wait()
+
+    ghost_index = [
+        lanes_at(map_low[0].astype(jnp.int32), low_names),
+        lanes_at(map_high[0].astype(jnp.int32), high_names),
+    ]
+    from_low_index = lanes_at(lower_map, map_low[1].astype(jnp.int32))
+    from_high_index = lanes_at(upper_map, map_high[1].astype(jnp.int32))
+    low_terms, _ = geometry(low_corner)
+    high_terms, _ = geometry(high_corner)
+
+    def outgoing(terms, k, turned, adjoint, j):
+        face_normal, face_area = terms[:2]
+        return (
+            face_normal[k][0] * turned[0][j]
+            + face_normal[k][1] * turned[1][j]
+            + face_normal[k][2] * turned[2][j]
+            - face_area[k] * adjoint[j]
+        )
+
+    def update_inside(terms, turned, adjoint, objective, j):
+        _, _, half_total, self_area, freq_volume, _ = terms
+        t, v = j // VARS, j % VARS
+        update = (
+            half_total[0] * turned[0][j]
+            + half_total[1] * turned[1][j]
+            + half_total[2] * turned[2][j]
+            + self_area * adjoint[j]
+            + objective[1, j]
+        )
+        mix = None
+        for other in range(INST):
+            if other != t:
+                term = float(spectral[other, t]) * adjoint[other * VARS + v]
+                mix = term if mix is None else mix + term
+        update = update + freq_volume * mix
+        update = update + pltpu.roll(outgoing(terms, 3, turned, adjoint, j), 4, 1)
+        update = update + pltpu.roll(outgoing(terms, 2, turned, adjoint, j), LANES - 4, 1)
+        update = update + pltpu.roll(outgoing(terms, 5, turned, adjoint, j), 1, 1)
+        return update + pltpu.roll(outgoing(terms, 4, turned, adjoint, j), LANES - 1, 1)
+
+    def sweep_blocks(neighbours_too):
+        own = [lattice[0, j] for j in range(STATE)]
+        own_turned = turn(own)
+        own_up = [pltpu.roll(outgoing(own_terms, 1, own_turned, own, j), 2, 0) for j in range(STATE)]
+        own_down = [pltpu.roll(outgoing(own_terms, 0, own_turned, own, j), 6, 0) for j in range(STATE)]
+
+        low = [low_state[0, j] for j in range(STATE)]
+        low_turned = turn(low)
+        low_up = [pltpu.roll(outgoing(low_terms, 1, low_turned, low, j), 2, 0) for j in range(STATE)]
+        if neighbours_too:
+            for j in range(STATE):
+                near = jnp.where(layer == 0, 0.0, low_up[j])
+                down = pltpu.roll(outgoing(low_terms, 0, low_turned, low, j), 6, 0)
+                near = near + jnp.where(layer == 3, lanes_at(own_down[j], from_low_index), down)
+                update = update_inside(low_terms, low_turned, low, low_state, j) + near
+                low_state[0, j] = low[j] - low_terms[5] * update
+
+        high = [high_state[0, j] for j in range(STATE)]
+        high_turned = turn(high)
+        high_down = [
+            pltpu.roll(outgoing(high_terms, 0, high_turned, high, j), 6, 0) for j in range(STATE)
+        ]
+        if neighbours_too:
+            for j in range(STATE):
+                near = jnp.where(layer == 3, 0.0, high_down[j])
+                up = pltpu.roll(outgoing(high_terms, 1, high_turned, high, j), 2, 0)
+                near = near + jnp.where(layer == 0, lanes_at(own_up[j], from_high_index), up)
+                update = update_inside(high_terms, high_turned, high, high_state, j) + near
+                high_state[0, j] = high[j] - high_terms[5] * update
+
+        for j in range(STATE):
+            near = jnp.where(layer == 0, lanes_at(low_up[j], ghost_index[0]), own_up[j])
+            near = near + jnp.where(layer == 3, lanes_at(high_down[j], ghost_index[1]), own_down[j])
+            update = update_inside(own_terms, own_turned, own, lattice, j) + near
+            lattice[0, j] = own[j] - own_terms[5] * update
+
+    def body(sweep, carry):
+        sweep_blocks(True)
+        return carry
+
+    lax.fori_loop(0, ITERS - 1, body, 0)
+    sweep_blocks(False)
     adjoint = [lattice[0, j] for j in range(STATE)]
-    for sweep in range(ITERS):
-        turned = turn(adjoint)
-
-        def outgoing(k, j):
-            return (
-                face_normal[k][0] * turned[0][j]
-                + face_normal[k][1] * turned[1][j]
-                + face_normal[k][2] * turned[2][j]
-                - face_area[k] * adjoint[j]
-            )
-
-        upward = [outgoing(1, j) for j in range(STATE)]
-        downward = [outgoing(0, j) for j in range(STATE)]
-        fill(sweep, upward, downward)
-        pair = exchange(sweep)
-        if sweep == 0:
-            moved_late = move_cells(stack_late[...], onehot, 1)
-            to_lattice(1, moved_late, 0)
-            to_lattice(2, moved_late, 50)
-            flow = [lattice[2, j] for j in range(STATE)]
-            fill(ITERS, flow, flow)
-            flow_pair = exchange(ITERS)
-        updates = []
-        for j in range(STATE):
-            t, v = j // VARS, j % VARS
-            update = (
-                half_total[0] * turned[0][j]
-                + half_total[1] * turned[1][j]
-                + half_total[2] * turned[2][j]
-                + self_area * adjoint[j]
-                + lattice[1, j]
-            )
-            mix = None
-            for other in range(INST):
-                if other != t:
-                    term = float(spectral[other, t]) * adjoint[other * VARS + v]
-                    mix = term if mix is None else mix + term
-            update = update + freq_volume * mix
-            update = update + pltpu.roll(outgoing(3, j), 4, 1)
-            update = update + pltpu.roll(outgoing(2, j), LANES - 4, 1)
-            update = update + pltpu.roll(outgoing(5, j), 1, 1)
-            update = update + pltpu.roll(outgoing(4, j), LANES - 1, 1)
-            update = update + jnp.where(layer == 0, 0.0, pltpu.roll(upward[j], 2, 0))
-            update = update + jnp.where(layer == 3, 0.0, pltpu.roll(downward[j], 6, 0))
-            updates.append(adjoint[j] - step * update)
-        for copy in pair:
-            copy.wait()
-        if sweep == 0:
-            for side in range(2):
-                table = (low_recv, high_recv)[side][0, GROUPS].astype(jnp.int32)
-                tile = 3 * side
-                row = moved[80 + side : 81 + side, tile * LANES : (tile + 1) * LANES]
-                named = spread(row.astype(jnp.int32)) - CELLS_HERE - side * LANES
-                ghost_index[side] = lanes_at(table, jnp.clip(named, 0, LANES - 1))
-        low, high = ghosts(sweep)
-        adjoint = [
-            updates[j] - step * jnp.where(layer == 0, low[j], jnp.where(layer == 3, high[j], 0.0))
-            for j in range(STATE)
-        ]
-
-    for copy in flow_pair:
-        copy.wait()
-
-    low, high = ghosts(ITERS)
+
+    low, high = ghosts()
     final_rows = turn(adjoint)
     along = [[None] * 3 for _ in range(6)]
     spread_sum = [None] * 6
@@ -563,7 +611,10 @@
         return x.transpose(1, 2, 0, 3).reshape(STATE, OPS_HERE, CELLS_HERE)
 
     rows = pltpu.VMEM((STATE, OPS_HERE, CELLS_HERE), f32)
-    message = pltpu.VMEM((ITERS + 1, GROUPS + 1, 8, LANES), f32)
+    message = pltpu.VMEM((GROUPS, 8, LANES), f32)
+    maps = pltpu.VMEM((2, 8, LANES), f32)
+    block = pltpu.VMEM((2, STATE, 8, LANES), f32)
+    points = pltpu.VMEM((3, 8, 8, LANES), f32)
     adjoint, sens = pl.pallas_call(
         kernel,
         out_shape=(
@@ -595,6 +646,14 @@
             message,
             message,
             message,
+            maps,
+            maps,
+            maps,
+            maps,
+            block,
+            block,
+            points,
+            points,
             pltpu.VMEM((N_OP, 8, LANES), f32),
             pltpu.VMEM((N_OP - 1, 8, LANES), f32),
             pltpu.VMEM((56, CELLS_HERE), f32),
@@ -604,10 +663,10 @@
             dma((3,)),
             dma((3,)),
             dma((3,)),
-            dma((ITERS + 1,)),
-            dma((ITERS + 1,)),
-            dma((ITERS + 1,)),
-            dma((ITERS + 1,)),
+            dma((5,)),
+            dma((5,)),
+            dma((5,)),
+            dma((5,)),
         ],
         compiler_params=pltpu.CompilerParams(collective_id=0, has_side_effects=True),
     )(

time: 51.8 us -> 40.1 us (0.77)
  Pallas kernels: 48.9 us -> 37.2 us
    pallas_call x1, Pallas kernels: 48.9 us -> 37.2 us  [per_device(): pl.pallas_call(kernel, out_shape=(jax.ShapeDtypeStruct((STATE, OPS_HERE,...]
where the time goes in v2:
time: 40.1 us; the launch traced here: 40 us
  Pallas kernels  37.2 us (93%)
  local copies, waits for them, and re-layouts  2.14 us (5%)
  between operations  0.65 us (2%)
    pallas_call x1, Pallas kernels, per_device(): pl.pallas_call(kernel, out_shape=(jax.ShapeDtypeStruct((STATE, OPS_HERE,...  37.2 us
    unnamed x4, local copies, waits for them, and re-layouts  2.14 us

profile of v2, /device:TPU:1, one launch (start us, length us, event | category | flops | bytes accessed | tf_op | source)
XLA Modules:
  0.0 40.0 jit_solution(636908349128590590)
XLA Ops:
  0.6 37.2 %shard_map.113 = (f32[25,2,512]{2,1,0:T(2,128)}, f32[3,256]{1,0:T(4,128)}) custom-call(f32[25,2,512]{2,1,0:T(2,128)} %bitcast.14, f32[25,2,512]{2,1,0:T(2,128)} %bitcast.15, f32[25,2,512]{2,1,0:T(2,128)} %bitcast.16, s32[6,512]{1,0:T(8,128)} %adjacency_in.1, s32[2,128]{1,0:T(2,128)} %bitcast.19, s32[8,512]{1,0:T(8,128)} %nodes_in.1, f32[3,256]{1,0:T(4,128)} %coords_in.1, ...), custom_call_target="tpu_custom_call" | custom-call | tf_op jit(solution)/shard_map/pallas_call | solution.py:618
  37.8 0.0 copy-start
  37.8 1.5 %copy.14 = f32[2,5,5,512]{3,0,2,1:T(2,128)} copy(f32[2,5,5,512]{3,0,2,1:T(2,128)} %bitcast.17) | data formatting | bytes 204800
  39.4 0.0 copy-done
  39.4 0.6 %copy.15 = f32[3,256]{1,0:T(4,128)} copy(f32[3,256]{1,0:T(4,128)S(1)} %copy-done) | data formatting | bytes 6144
Async XLA Ops:
  37.8 1.6 %copy-start = (f32[3,256]{1,0:T(4,128)S(1)}, f32[3,256]{1,0:T(4,128)}, u32[]{:S(2)}) copy-start(f32[3,256]{1,0:T(4,128)} %get-tuple-element.9) | copy-start | bytes 9220

commit v3 on v2

--- a/solution.py
+++ b/solution.py
@@ -104,6 +104,7 @@
     high_state,
     low_corner,
     high_corner,
+    first_part,
     rs_send,
     rs_recv,
     outbuf,
@@ -370,7 +371,56 @@
             for d in range(3)
         ]
 
-    for copy in copies:
+    def outgoing(terms, k, turned, adjoint, j):
+        face_normal, face_area = terms[:2]
+        return (
+            face_normal[k][0] * turned[0][j]
+            + face_normal[k][1] * turned[1][j]
+            + face_normal[k][2] * turned[2][j]
+            - face_area[k] * adjoint[j]
+        )
+
+    def faces(terms, adjoint):
+        turned = turn(adjoint)
+        up = [pltpu.roll(outgoing(terms, 1, turned, adjoint, j), 2, 0) for j in range(STATE)]
+        down = [pltpu.roll(outgoing(terms, 0, turned, adjoint, j), 6, 0) for j in range(STATE)]
+        return turned, up, down
+
+    def inside(terms, turned, adjoint, objective):
+        _, _, half_total, self_area, freq_volume, _ = terms
+        updates = []
+        for j in range(STATE):
+            t, v = j // VARS, j % VARS
+            update = (
+                half_total[0] * turned[0][j]
+                + half_total[1] * turned[1][j]
+                + half_total[2] * turned[2][j]
+                + self_area * adjoint[j]
+                + objective(j)
+            )
+            mix = None
+            for other in range(INST):
+                if other != t:
+                    term = float(spectral[other, t]) * adjoint[other * VARS + v]
+                    mix = term if mix is None else mix + term
+            update = update + freq_volume * mix
+            update = update + pltpu.roll(outgoing(terms, 3, turned, adjoint, j), 4, 1)
+            update = update + pltpu.roll(outgoing(terms, 2, turned, adjoint, j), LANES - 4, 1)
+            update = update + pltpu.roll(outgoing(terms, 5, turned, adjoint, j), 1, 1)
+            update = update + pltpu.roll(outgoing(terms, 4, turned, adjoint, j), LANES - 1, 1)
+            updates.append(update)
+        return updates
+
+    def advance(terms, adjoint, updates, near):
+        return [adjoint[j] - terms[5] * (updates[j] + near(j)) for j in range(STATE)]
+
+    own = [lattice[0, j] for j in range(STATE)]
+    own_turned, own_up, own_down = faces(own_terms, own)
+    own_part = inside(own_terms, own_turned, own, lambda j: lattice[1, j])
+    for j in range(STATE):
+        first_part[j] = own_part[j]
+
+    for copy in copies[:6]:
         copy.wait()
 
     ghost_index = [
@@ -381,80 +431,77 @@
     from_high_index = lanes_at(upper_map, map_high[1].astype(jnp.int32))
     low_terms, _ = geometry(low_corner)
     high_terms, _ = geometry(high_corner)
-
-    def outgoing(terms, k, turned, adjoint, j):
-        face_normal, face_area = terms[:2]
-        return (
-            face_normal[k][0] * turned[0][j]
-            + face_normal[k][1] * turned[1][j]
-            + face_normal[k][2] * turned[2][j]
-            - face_area[k] * adjoint[j]
-        )
-
-    def update_inside(terms, turned, adjoint, objective, j):
-        _, _, half_total, self_area, freq_volume, _ = terms
-        t, v = j // VARS, j % VARS
-        update = (
-            half_total[0] * turned[0][j]
-            + half_total[1] * turned[1][j]
-            + half_total[2] * turned[2][j]
-            + self_area * adjoint[j]
-            + objective[1, j]
-        )
-        mix = None
-        for other in range(INST):
-            if other != t:
-                term = float(spectral[other, t]) * adjoint[other * VARS + v]
-                mix = term if mix is None else mix + term
-        update = update + freq_volume * mix
-        update = update + pltpu.roll(outgoing(terms, 3, turned, adjoint, j), 4, 1)
-        update = update + pltpu.roll(outgoing(terms, 2, turned, adjoint, j), LANES - 4, 1)
-        update = update + pltpu.roll(outgoing(terms, 5, turned, adjoint, j), 1, 1)
-        return update + pltpu.roll(outgoing(terms, 4, turned, adjoint, j), LANES - 1, 1)
-
-    def sweep_blocks(neighbours_too):
-        own = [lattice[0, j] for j in range(STATE)]
-        own_turned = turn(own)
-        own_up = [pltpu.roll(outgoing(own_terms, 1, own_turned, own, j), 2, 0) for j in range(STATE)]
-        own_down = [pltpu.roll(outgoing(own_terms, 0, own_turned, own, j), 6, 0) for j in range(STATE)]
-
-        low = [low_state[0, j] for j in range(STATE)]
-        low_turned = turn(low)
-        low_up = [pltpu.roll(outgoing(low_terms, 1, low_turned, low, j), 2, 0) for j in range(STATE)]
-        if neighbours_too:
-            for j in range(STATE):
-                near = jnp.where(layer == 0, 0.0, low_up[j])
-                down = pltpu.roll(outgoing(low_terms, 0, low_turned, low, j), 6, 0)
-                near = near + jnp.where(layer == 3, lanes_at(own_down[j], from_low_index), down)
-                update = update_inside(low_terms, low_turned, low, low_state, j) + near
-                low_state[0, j] = low[j] - low_terms[5] * update
-
-        high = [high_state[0, j] for j in range(STATE)]
-        high_turned = turn(high)
-        high_down = [
-            pltpu.roll(outgoing(high_terms, 0, high_turned, high, j), 6, 0) for j in range(STATE)
-        ]
-        if neighbours_too:
-            for j in range(STATE):
-                near = jnp.where(layer == 3, 0.0, high_down[j])
-                up = pltpu.roll(outgoing(high_terms, 1, high_turned, high, j), 2, 0)
-                near = near + jnp.where(layer == 0, lanes_at(own_up[j], from_high_index), up)
-                update = update_inside(high_terms, high_turned, high, high_state, j) + near
-                high_state[0, j] = high[j] - high_terms[5] * update
-
-        for j in range(STATE):
-            near = jnp.where(layer == 0, lanes_at(low_up[j], ghost_index[0]), own_up[j])
-            near = near + jnp.where(layer == 3, lanes_at(high_down[j], ghost_index[1]), own_down[j])
-            update = update_inside(own_terms, own_turned, own, lattice, j) + near
-            lattice[0, j] = own[j] - own_terms[5] * update
-
-    def body(sweep, carry):
-        sweep_blocks(True)
-        return carry
-
-    lax.fori_loop(0, ITERS - 1, body, 0)
-    sweep_blocks(False)
-    adjoint = [lattice[0, j] for j in range(STATE)]
+    low = [low_state[0, j] for j in range(STATE)]
+    high = [high_state[0, j] for j in range(STATE)]
+    for copy in copies[6:8]:
+        copy.wait()
+
+    for sweep in range(2):
+        if sweep > 0:
+            own_turned, own_up, own_down = faces(own_terms, own)
+            own_part = inside(own_terms, own_turned, own, lambda j: lattice[1, j])
+        else:
+            own_part = [first_part[j] for j in range(STATE)]
+        low_turned, low_up, low_down = faces(low_terms, low)
+        low_part = inside(low_terms, low_turned, low, lambda j: low_state[1, j])
+        low = advance(
+            low_terms,
+            low,
+            low_part,
+            lambda j: jnp.where(layer == 0, 0.0, low_up[j])
+            + jnp.where(layer == 3, lanes_at(own_down[j], from_low_index), low_down[j]),
+        )
+        high_turned, high_up, high_down = faces(high_terms, high)
+        high_part = inside(high_terms, high_turned, high, lambda j: high_state[1, j])
+        high = advance(
+            high_terms,
+            high,
+            high_part,
+            lambda j: jnp.where(layer == 3, 0.0, high_down[j])
+            + jnp.where(layer == 0, lanes_at(own_up[j], from_high_index), high_up[j]),
+        )
+        own = advance(
+            own_terms,
+            own,
+            own_part,
+            lambda j: jnp.where(layer == 0, lanes_at(low_up[j], ghost_index[0]), own_up[j])
+            + jnp.where(layer == 3, lanes_at(high_down[j], ghost_index[1]), own_down[j]),
+        )
+
+    def halves(x, y):
+        if isinstance(x, (tuple, list)):
+            return [halves(a, b) for a, b in zip(x, y)]
+        return jnp.where(layer >= 2, x, y)
+
+    outer, outer_terms = halves(low, high), halves(low_terms, high_terms)
+    for sweep in range(2, ITERS):
+        own_turned, own_up, own_down = faces(own_terms, own)
+        outer_turned, outer_up, outer_down = faces(outer_terms, outer)
+        own_part = inside(own_terms, own_turned, own, lambda j: lattice[1, j])
+        own = advance(
+            own_terms,
+            own,
+            own_part,
+            lambda j: jnp.where(layer == 0, lanes_at(outer_up[j], ghost_index[0]), own_up[j])
+            + jnp.where(layer == 3, lanes_at(outer_down[j], ghost_index[1]), own_down[j]),
+        )
+        if sweep < ITERS - 1:
+            outer_part = inside(
+                outer_terms,
+                outer_turned,
+                outer,
+                lambda j: halves(low_state[1, j], high_state[1, j]),
+            )
+            outer = advance(
+                outer_terms,
+                outer,
+                outer_part,
+                lambda j: jnp.where(layer == 0, lanes_at(own_up[j], from_high_index), outer_up[j])
+                + jnp.where(layer == 3, lanes_at(own_down[j], from_low_index), outer_down[j]),
+            )
+    adjoint = own
+    for copy in copies[8:]:
+        copy.wait()
 
     low, high = ghosts()
     final_rows = turn(adjoint)
@@ -654,6 +701,7 @@
             block,
             points,
             points,
+            pltpu.VMEM((STATE, 8, LANES), f32),
             pltpu.VMEM((N_OP, 8, LANES), f32),
             pltpu.VMEM((N_OP - 1, 8, LANES), f32),
             pltpu.VMEM((56, CELLS_HERE), f32),

time: 40.1 us -> 38.5 us (0.960)
  Pallas kernels: 37.2 us -> 35.5 us
    pallas_call x1, Pallas kernels: 37.2 us -> 35.5 us  [per_device(): pl.pallas_call(kernel, out_shape=(jax.ShapeDtypeStruct((STATE, OPS_HERE,...]
where the time goes in v3:
time: 38.5 us; the launch traced here: 38.3 us
  Pallas kernels  35.5 us (92%)
  local copies, waits for them, and re-layouts  2.14 us (6%)
  between operations  0.65 us (2%)
    pallas_call x1, Pallas kernels, per_device(): pl.pallas_call(kernel, out_shape=(jax.ShapeDtypeStruct((STATE, OPS_HERE,...  35.5 us
    unnamed x4, local copies, waits for them, and re-layouts  2.14 us

profile of v3, /device:TPU:1, one launch (start us, length us, event | category | flops | bytes accessed | tf_op | source)
XLA Modules:
  0.0 38.3 jit_solution(13193884536638896539)
XLA Ops:
  0.6 35.5 %shard_map.113 = (f32[25,2,512]{2,1,0:T(2,128)}, f32[3,256]{1,0:T(4,128)}) custom-call(f32[25,2,512]{2,1,0:T(2,128)} %bitcast.14, f32[25,2,512]{2,1,0:T(2,128)} %bitcast.15, f32[25,2,512]{2,1,0:T(2,128)} %bitcast.16, s32[6,512]{1,0:T(8,128)} %adjacency_in.1, s32[2,128]{1,0:T(2,128)} %bitcast.19, s32[8,512]{1,0:T(8,128)} %nodes_in.1, f32[3,256]{1,0:T(4,128)} %coords_in.1, ...), custom_call_target="tpu_custom_call" | custom-call | tf_op jit(solution)/shard_map/pallas_call | solution.py:665
  36.2 0.0 copy-start
  36.2 1.5 %copy.14 = f32[2,5,5,512]{3,0,2,1:T(2,128)} copy(f32[2,5,5,512]{3,0,2,1:T(2,128)} %bitcast.17) | data formatting | bytes 204800
  37.7 0.0 copy-done
  37.7 0.6 %copy.15 = f32[3,256]{1,0:T(4,128)} copy(f32[3,256]{1,0:T(4,128)S(1)} %copy-done) | data formatting | bytes 6144
Async XLA Ops:
  36.2 1.6 %copy-start = (f32[3,256]{1,0:T(4,128)S(1)}, f32[3,256]{1,0:T(4,128)}, u32[]{:S(2)}) copy-start(f32[3,256]{1,0:T(4,128)} %get-tuple-element.9) | copy-start | bytes 9220

commit v4 on v3

--- a/solution.py
+++ b/solution.py
@@ -105,6 +105,9 @@
     low_corner,
     high_corner,
     first_part,
+    corner_pack,
+    low_pack,
+    high_pack,
     rs_send,
     rs_recv,
     outbuf,
@@ -237,6 +240,7 @@
             part = moved[56 + 8 * d : 64 + 8 * d, l * LANES : (l + 1) * LANES]
             corner_lat[d, :, 2 * l, :] = part
             corner_lat[d, :, 2 * l + 1, :] = part
+            corner_pack[d, :, l, :] = part
         slot_lat[:, l, :] = moved[88:96, l * LANES : (l + 1) * LANES]
 
     def pos_of(cells):
@@ -297,9 +301,9 @@
     map_up[1] = high_names.astype(jnp.float32)
     map_down[0] = lower_map.astype(jnp.float32)
     map_down[1] = low_names.astype(jnp.float32)
-    exchange(0, lattice.at[0], low_state.at[0], lattice.at[0], high_state.at[0])
-    exchange(1, corner_lat, low_corner, corner_lat, high_corner)
-    exchange(2, map_up, map_low, map_down, map_high)
+    exchange(0, corner_pack, low_pack, corner_pack, high_pack)
+    exchange(1, map_up, map_low, map_down, map_high)
+    exchange(2, lattice.at[0], low_state.at[0], lattice.at[0], high_state.at[0])
     moved_late = move_cells(stack_late[...], onehot, 1)
     to_lattice(1, moved_late, 0)
     exchange(3, lattice.at[1], low_state.at[1], lattice.at[1], high_state.at[1])
@@ -420,8 +424,31 @@
     for j in range(STATE):
         first_part[j] = own_part[j]
 
-    for copy in copies[:6]:
+    limits = (4, 32, 4)
+    point = [
+        jnp.clip(jnp.floor(jnp.clip(nodebuf[d], -1.0, 40.0) + 0.5).astype(jnp.int32), 0, limits[d])
+        for d in range(3)
+    ]
+    home = [jnp.minimum(point[d], limits[d] - 1) for d in range(3)]
+    source = ((point[0] - home[0]) * 4 + (point[1] - home[1]) * 2 + point[2] - home[2]) * 4 + home[0]
+    within = home[1] * 4 + home[2]
+    slot_number = (sub * LANES + lane).astype(jnp.float32)
+    name = jnp.full((8, LANES), -1.0, jnp.float32)
+    for c in range(8):
+        slots = slot_lat[c]
+        for l in range(4):
+            got = lanes_at(spread(slots[l : l + 1]), within)
+            name = jnp.where(source == c * 4 + l, got, name)
+    source = jnp.where(name == slot_number, source, -1)
+
+    for copy in copies[:4]:
         copy.wait()
+    for pack_ref, full_ref in ((low_pack, low_corner), (high_pack, high_corner)):
+        for d in range(3):
+            for l in range(4):
+                part = pack_ref[d, :, l, :]
+                full_ref[d, :, 2 * l, :] = part
+                full_ref[d, :, 2 * l + 1, :] = part
 
     ghost_index = [
         lanes_at(map_low[0].astype(jnp.int32), low_names),
@@ -431,6 +458,8 @@
     from_high_index = lanes_at(upper_map, map_high[1].astype(jnp.int32))
     low_terms, _ = geometry(low_corner)
     high_terms, _ = geometry(high_corner)
+    for copy in copies[4:6]:
+        copy.wait()
     low = [low_state[0, j] for j in range(STATE)]
     high = [high_state[0, j] for j in range(STATE)]
     for copy in copies[6:8]:
@@ -582,21 +611,10 @@
     meet(2, lambda x: pltpu.roll(x, 4, 1), lambda x: pltpu.roll(x, LANES - 4, 1), lane < 4, lane >= LANES - 4)
     meet(4, lambda x: pltpu.roll(x, 2, 0), lambda x: pltpu.roll(x, 6, 0), layer == 0, layer == 3)
 
-    limits = (4, 32, 4)
-    point = [
-        jnp.clip(jnp.floor(jnp.clip(nodebuf[d], -1.0, 40.0) + 0.5).astype(jnp.int32), 0, limits[d])
-        for d in range(3)
-    ]
-    home = [jnp.minimum(point[d], limits[d] - 1) for d in range(3)]
-    source = ((point[0] - home[0]) * 4 + (point[1] - home[1]) * 2 + point[2] - home[2]) * 4 + home[0]
-    within = home[1] * 4 + home[2]
-    slot_number = sub * LANES + lane
     sens = [jnp.zeros((8, LANES), jnp.float32) for _ in range(3)]
     for c in range(8):
-        slots = slot_lat[c]
         for l in range(4):
-            name = lanes_at(spread(slots[l : l + 1]), within).astype(jnp.int32)
-            chosen = jnp.logical_and(source == c * 4 + l, name == slot_number)
+            chosen = source == c * 4 + l
             for d in range(3):
                 got = lanes_at(spread(cots[c][d][2 * l : 2 * l + 1]), within)
                 sens[d] = jnp.where(chosen, got, sens[d])
@@ -662,6 +680,7 @@
     maps = pltpu.VMEM((2, 8, LANES), f32)
     block = pltpu.VMEM((2, STATE, 8, LANES), f32)
     points = pltpu.VMEM((3, 8, 8, LANES), f32)
+    packed = pltpu.VMEM((3, 8, 4, LANES), f32)
     adjoint, sens = pl.pallas_call(
         kernel,
         out_shape=(
@@ -702,6 +721,9 @@
             points,
             points,
             pltpu.VMEM((STATE, 8, LANES), f32),
+            packed,
+            packed,
+            packed,
             pltpu.VMEM((N_OP, 8, LANES), f32),
             pltpu.VMEM((N_OP - 1, 8, LANES), f32),
             pltpu.VMEM((56, CELLS_HERE), f32),

time: 38.5 us -> 37.4 us (0.971)
  Pallas kernels: 35.5 us -> 34.5 us
    pallas_call x1, Pallas kernels: 35.5 us -> 34.5 us  [per_device(): pl.pallas_call(kernel, out_shape=(jax.ShapeDtypeStruct((STATE, OPS_HERE,...]
where the time goes in v4:
time: 37.4 us; the launch traced here: 37.3 us
  Pallas kernels  34.5 us (92%)
  local copies, waits for them, and re-layouts  2.14 us (6%)
  between operations  0.65 us (2%)
    pallas_call x1, Pallas kernels, per_device(): pl.pallas_call(kernel, out_shape=(jax.ShapeDtypeStruct((STATE, OPS_HERE,...  34.5 us
    unnamed x4, local copies, waits for them, and re-layouts  2.14 us

profile of v4, /device:TPU:1, one launch (start us, length us, event | category | flops | bytes accessed | tf_op | source)
XLA Modules:
  0.0 37.3 jit_solution(5499036708087468748)
XLA Ops:
  0.6 34.5 %shard_map.113 = (f32[25,2,512]{2,1,0:T(2,128)}, f32[3,256]{1,0:T(4,128)}) custom-call(f32[25,2,512]{2,1,0:T(2,128)} %bitcast.14, f32[25,2,512]{2,1,0:T(2,128)} %bitcast.15, f32[25,2,512]{2,1,0:T(2,128)} %bitcast.16, s32[6,512]{1,0:T(8,128)} %adjacency_in.1, s32[2,128]{1,0:T(2,128)} %bitcast.19, s32[8,512]{1,0:T(8,128)} %nodes_in.1, f32[3,256]{1,0:T(4,128)} %coords_in.1, ...), custom_call_target="tpu_custom_call" | custom-call | tf_op jit(solution)/shard_map/pallas_call | solution.py:684
  35.1 0.0 copy-start
  35.1 1.5 %copy.14 = f32[2,5,5,512]{3,0,2,1:T(2,128)} copy(f32[2,5,5,512]{3,0,2,1:T(2,128)} %bitcast.17) | data formatting | bytes 204800
  36.7 0.0 copy-done
  36.7 0.6 %copy.15 = f32[3,256]{1,0:T(4,128)} copy(f32[3,256]{1,0:T(4,128)S(1)} %copy-done) | data formatting | bytes 6144
Async XLA Ops:
  35.1 1.6 %copy-start = (f32[3,256]{1,0:T(4,128)S(1)}, f32[3,256]{1,0:T(4,128)}, u32[]{:S(2)}) copy-start(f32[3,256]{1,0:T(4,128)} %get-tuple-element.9) | copy-start | bytes 9220

commit v5 on v4

--- a/solution.py
+++ b/solution.py
@@ -197,7 +197,7 @@
     freq = pick(freq_ref[0], freq_ref[1])
 
     for copy in coord_copies:
-        copy.wait()
+        copy.wait_recv()
 
     for o in range(N_OP):
         for d in range(3):
@@ -442,7 +442,7 @@
     source = jnp.where(name == slot_number, source, -1)
 
     for copy in copies[:4]:
-        copy.wait()
+        copy.wait_recv()
     for pack_ref, full_ref in ((low_pack, low_corner), (high_pack, high_corner)):
         for d in range(3):
             for l in range(4):
@@ -459,11 +459,11 @@
     low_terms, _ = geometry(low_corner)
     high_terms, _ = geometry(high_corner)
     for copy in copies[4:6]:
-        copy.wait()
+        copy.wait_recv()
     low = [low_state[0, j] for j in range(STATE)]
     high = [high_state[0, j] for j in range(STATE)]
     for copy in copies[6:8]:
-        copy.wait()
+        copy.wait_recv()
 
     for sweep in range(2):
         if sweep > 0:
@@ -530,7 +530,7 @@
             )
     adjoint = own
     for copy in copies[8:]:
-        copy.wait()
+        copy.wait_recv()
 
     low, high = ghosts()
     final_rows = turn(adjoint)
@@ -653,6 +653,8 @@
     for d in range(3):
         for h in range(2):
             sens_ref[d : d + 1, h * LANES : (h + 1) * LANES] = total[2 * d + h : 2 * d + h + 1]
+    for copy in coord_copies + copies:
+        copy.wait_send()
     put.wait()
 
 

time: 37.4 us -> 37.4 us (level)
  no operation moved by 1% of the time
where the time goes in v5:
time: 37.4 us; the launch traced here: 37.3 us
  Pallas kernels  34.5 us (92%)
  local copies, waits for them, and re-layouts  2.14 us (6%)
  between operations  0.65 us (2%)
    pallas_call x1, Pallas kernels, per_device(): pl.pallas_call(kernel, out_shape=(jax.ShapeDtypeStruct((STATE, OPS_HERE,...  34.5 us
    unnamed x4, local copies, waits for them, and re-layouts  2.14 us

profile of v5, /device:TPU:1, one launch (start us, length us, event | category | flops | bytes accessed | tf_op | source)
XLA Modules:
  0.0 37.3 jit_solution(15316292404734603387)
XLA Ops:
  0.6 34.5 %shard_map.113 = (f32[25,2,512]{2,1,0:T(2,128)}, f32[3,256]{1,0:T(4,128)}) custom-call(f32[25,2,512]{2,1,0:T(2,128)} %bitcast.14, f32[25,2,512]{2,1,0:T(2,128)} %bitcast.15, f32[25,2,512]{2,1,0:T(2,128)} %bitcast.16, s32[6,512]{1,0:T(8,128)} %adjacency_in.1, s32[2,128]{1,0:T(2,128)} %bitcast.19, s32[8,512]{1,0:T(8,128)} %nodes_in.1, f32[3,256]{1,0:T(4,128)} %coords_in.1, ...), custom_call_target="tpu_custom_call" | custom-call | tf_op jit(solution)/shard_map/pallas_call | solution.py:686
  35.1 0.0 copy-start
  35.1 1.5 %copy.14 = f32[2,5,5,512]{3,0,2,1:T(2,128)} copy(f32[2,5,5,512]{3,0,2,1:T(2,128)} %bitcast.17) | data formatting | bytes 204800
  36.7 0.0 copy-done
  36.7 0.6 %copy.15 = f32[3,256]{1,0:T(4,128)} copy(f32[3,256]{1,0:T(4,128)S(1)} %copy-done) | data formatting | bytes 6144
Async XLA Ops:
  35.1 1.6 %copy-start = (f32[3,256]{1,0:T(4,128)S(1)}, f32[3,256]{1,0:T(4,128)}, u32[]{:S(2)}) copy-start(f32[3,256]{1,0:T(4,128)} %get-tuple-element.9) | copy-start | bytes 9220
